TPU v7x, 32 devices: a whole 2x2x4 slice. The times are simulated.
32 devices in a mesh: expert: 16 (over z, y, x), fsdp: 2 (over core).
Axes of the slice: x: 2, y: 2, z: 4, core: 2. Of those that a mesh axis runs over, the one named last changes fastest.
Arguments:
- tokens: bfloat16 [4096, 512], P(('expert', 'fsdp')), may hold values from -6 to 6
- out_grad: bfloat16 [4096, 512], P(('expert', 'fsdp')), may hold values from -6 to 6
- gates: bfloat16 [4096, 2], P('expert'), may hold values from 0.099609375 to 1
- expert_ids: int32 [4096, 2], P('expert'), may hold values from 0 to 15, as said below
- w_in: bfloat16 [16, 512, 4096], P('expert', None, 'fsdp'), may hold values from -0.25 to 0.25
- w_out: bfloat16 [16, 512, 4096], P('expert', None, 'fsdp'), may hold values from -0.09375 to 0.09375
Outputs:
- d_tokens: bfloat16 [4096, 512], P(('expert', 'fsdp'))
- d_gates: float32 [4096, 2], P(('expert', 'fsdp'))
- d_w_in: bfloat16 [16, 512, 4096], P('expert', None, 'fsdp')
- d_w_out: bfloat16 [16, 512, 4096], P('expert', None, 'fsdp')
Inputs may be any that keep to these rules, and one draw needn't show every extreme that they name: `expert_ids`: each token names two different experts. Within each aligned block of 128 tokens (the tokens of one device) no expert is named more than 20 times, and in every block some expert is named exactly 20 times.
All inputs are finite; a program needn't handle non-finite values.
Results may differ from a plain program's by a relative error of at most 0.011.
Values may be sent and summed in bfloat16 or wider, within the bound.
No kernel may reach another device: no remote copies, remote signals or barrier semaphores. Data moves between devices by JAX's collectives and lax.ppermute only.
A program may use at most 64 MiB of HBM per device.

v0:
```python
import jax
import jax.numpy as jnp
from jax import lax
from jax.sharding import PartitionSpec as P

COEF = 0.7978845608
CUBIC = 0.044715
ROW_DIMS = (((0,), (0,)), ((), ()))
LAST_DIMS = (((1,), (1,)), ((), ()))


def gelu_parts(pre_act):
    inner = COEF * (pre_act + CUBIC * pre_act * pre_act * pre_act)
    tangent = jnp.tanh(inner)
    values = 0.5 * pre_act * (1.0 + tangent)
    slopes = 0.5 * (1.0 + tangent) + 0.5 * pre_act * (1.0 - tangent * tangent) * COEF * (
        1.0 + 3.0 * CUBIC * pre_act * pre_act
    )
    return (values, slopes)


def slot_ranks(route_ids):
    count = route_ids.shape[1]
    same = route_ids[:, :, None] == route_ids[:, None, :]
    earlier = jnp.arange(count)[None, :] < jnp.arange(count)[:, None]
    return jnp.sum(jnp.logical_and(same, earlier[None]), axis=2)


def fill_slots(owner, rows_x, rows_dy, gate_flat):
    valid = owner >= 0
    safe = jnp.where(valid, owner, 0)
    token_row = safe // 2
    x_buf = jnp.where(valid[:, None], rows_x[token_row], jnp.zeros((), rows_x.dtype))
    dy_buf = jnp.where(valid[:, None], rows_dy[token_row], jnp.zeros((), rows_dy.dtype))
    gate_buf = jnp.where(valid, gate_flat[safe], jnp.zeros((), gate_flat.dtype))
    return (x_buf, dy_buf, gate_buf)


def expert_work(x_rows, dy_rows, gate_rows, in_shard, out_shard):
    pre_act = jnp.dot(x_rows, in_shard, preferred_element_type=jnp.float32)
    grad_act = jnp.dot(dy_rows, out_shard, preferred_element_type=jnp.float32)
    values, slopes = gelu_parts(pre_act)
    scale = gate_rows.astype(jnp.float32)[:, None]
    act_scaled = (scale * values).astype(jnp.bfloat16)
    grad_pre = (scale * grad_act * slopes).astype(jnp.bfloat16)
    grad_out = lax.dot_general(dy_rows, act_scaled, ROW_DIMS, preferred_element_type=jnp.float32)
    grad_in = lax.dot_general(x_rows, grad_pre, ROW_DIMS, preferred_element_type=jnp.float32)
    token_part = lax.dot_general(
        grad_pre, in_shard, LAST_DIMS, preferred_element_type=jnp.float32
    ).astype(jnp.bfloat16)
    gate_part = jnp.sum(grad_act * values, axis=1).astype(jnp.bfloat16)
    return (grad_in, grad_out, token_part, gate_part)


def per_device(tokens, out_grad, gates, expert_ids, w_in, w_out):
    tok_dev, width = tokens.shape
    groups = lax.axis_size("fsdp")
    experts = lax.axis_size("expert")
    capacity = 5 * tok_dev // (2 * experts)
    in_shard = w_in[0]
    out_shard = w_out[0]
    group_ids = expert_ids.reshape(groups, 2 * tok_dev)
    group_gates = gates.reshape(groups, 2 * tok_dev)
    group_ranks = slot_ranks(group_ids)
    all_x, all_dy = (
        lax.all_gather(tokens, "fsdp", axis=0, tiled=True),
        lax.all_gather(out_grad, "fsdp", axis=0, tiled=True),
    )
    member = jnp.arange(groups, dtype=jnp.int32)[:, None]
    target = ((group_ids * groups + member) * capacity + group_ranks).reshape(-1)
    owner = (
        jnp.full((experts * groups * capacity,), -1, jnp.int32)
        .at[target]
        .set(jnp.arange(2 * tok_dev * groups, dtype=jnp.int32))
    )
    x_buf, dy_buf, gate_buf = fill_slots(owner, all_x, all_dy, group_gates.reshape(-1))
    span = groups * capacity
    x_recv, dy_recv, gate_recv = (
        lax.all_to_all(
            x_buf.reshape(experts, span, width), "expert", split_axis=0, concat_axis=0, tiled=True
        ),
        lax.all_to_all(
            dy_buf.reshape(experts, span, width), "expert", split_axis=0, concat_axis=0, tiled=True
        ),
        lax.all_to_all(
            gate_buf.reshape(experts, span), "expert", split_axis=0, concat_axis=0, tiled=True
        ),
    )
    total_rows = experts * span
    grad_in, grad_out, token_part, gate_part = expert_work(
        x_recv.reshape(total_rows, width),
        dy_recv.reshape(total_rows, width),
        gate_recv.reshape(total_rows),
        in_shard,
        out_shard,
    )
    token_back, gate_back = (
        lax.all_to_all(
            token_part.reshape(experts, span, width),
            "expert",
            split_axis=0,
            concat_axis=0,
            tiled=True,
        ),
        lax.all_to_all(
            gate_part.reshape(experts, span), "expert", split_axis=0, concat_axis=0, tiled=True
        ),
    )
    token_pick = (
        token_back.reshape(total_rows, width)[target]
        .astype(jnp.float32)
        .reshape(groups * tok_dev, 2, width)
    )
    token_terms = jnp.sum(token_pick, axis=1)
    gate_terms = (
        gate_back.reshape(total_rows)[target].astype(jnp.float32).reshape(groups * tok_dev, 2)
    )
    token_sum, gate_sum = (
        lax.psum_scatter(
            token_terms.astype(jnp.bfloat16), "fsdp", scatter_dimension=0, tiled=True
        ).astype(jnp.float32),
        lax.psum_scatter(
            gate_terms.astype(jnp.bfloat16), "fsdp", scatter_dimension=0, tiled=True
        ).astype(jnp.float32),
    )
    return (
        token_sum.astype(jnp.bfloat16),
        gate_sum,
        grad_in.astype(jnp.bfloat16)[None],
        grad_out.astype(jnp.bfloat16)[None],
    )


def solution(mesh):
    return jax.shard_map(
        per_device,
        mesh=mesh,
        in_specs=(
            P(("expert", "fsdp"), None),
            P(("expert", "fsdp"), None),
            P("expert", None),
            P("expert", None),
            P("expert", None, "fsdp"),
            P("expert", None, "fsdp"),
        ),
        out_specs=(
            P(("expert", "fsdp"), None),
            P(("expert", "fsdp"), None),
            P("expert", None, "fsdp"),
            P("expert", None, "fsdp"),
        ),
        check_vma=False,
    )
```

profile of v0, /device:TPU:0, one launch (start us, length us, event | category | flops | bytes accessed | tf_op | source)
XLA Modules:
  0.0 149.8 jit_solution(11499161900919406336)
XLA Ops:
  7.2 1.0 copy.21
  8.2 0.7 broadcast_multiply_fusion
  9.0 0.3 convert_reduce_fusion
  9.6 2.4 %scatter_custom_fusion = s32[640]{0:T(1024)S(1)} fusion(s32[512]{0:T(512)S(1)} %bitcast.47, s32[512]{0:T(512)S(1)} %iota.22, s32[]{:T(128)} %constant.15.clone.1), kind=kCustom, calls=%fused_computation.50 | custom fusion | bytes 2564 | tf_op jit(solution)/shard_map/scatter | solution.py:74
  12.1 0.8 copy.22
  13.1 4.3 %gather_fusion = bf16[640]{0:T(1024)(128)(2,1)S(1)} fusion(bf16[512]{0:T(512)(128)(2,1)S(1)} %reshape_reshape.3, s32[1024]{0:T(1024)S(1)} %pad_clamp_fusion.2), kind=kCustom, calls=%fused_computation | custom fusion | bytes 5120 | tf_op jit(solution)/shard_map/gather | solution.py:35
  17.4 0.7 all_to_all.25
  18.1 8.3 %all-to-all-start = ((bf16[16,1,40]{2,1,0:T(2,128)(2,1)}), bf16[16,1,40]{2,1,0:T(2,128)(2,1)S(1)}, u32[]{:S(2)}, u32[]{:S(2)}) async-start(bf16[16,1,40]{2,1,0:T(2,128)(2,1)} %all_to_all.25), calls=%async_computation | async-start | bytes 16384 | tf_op jit(solution)/shard_map/all_to_all | solution.py:85
  26.6 2.2 %all_gather.7 = bf16[256,512]{1,0:T(8,128)(2,1)S(1)} all-gather(bf16[128,512]{1,0:T(8,128)(2,1)} %param.6), channel_id=1, replica_groups=mesh['expert'=16,'fsdp'=2] {'fsdp'}, dimensions={0}, use_global_device_ids=true | all-gather | bytes 393216 | tf_op jit(solution)/shard_map/all_gather | solution.py:66
  28.8 2.2 %all_gather.6 = bf16[256,512]{1,0:T(8,128)(2,1)S(1)} all-gather(bf16[128,512]{1,0:T(8,128)(2,1)} %param.7), channel_id=1, replica_groups=mesh['expert'=16,'fsdp'=2] {'fsdp'}, dimensions={0}, use_global_device_ids=true | all-gather | bytes 393216 | tf_op jit(solution)/shard_map/all_gather | solution.py:67
  31.0 2.8 %gather_fusion.2 = bf16[640,512]{1,0:T(8,128)(2,1)S(1)} fusion(bf16[256,512]{1,0:T(8,128)(2,1)S(1)} %all_gather.7, s32[1024]{0:T(1024)S(1)} %pad_clamp_fusion.1), kind=kCustom, calls=%fused_computation.2 | custom fusion | bytes 1313280 | tf_op jit(solution)/shard_map/gather | solution.py:33
  33.7 3.3 %gather_fusion.1 = bf16[640,512]{1,0:T(8,128)(2,1)} fusion(bf16[256,512]{1,0:T(8,128)(2,1)S(1)} %all_gather.6, s32[1024]{0:T(1024)S(1)} %pad_clamp_fusion.1), kind=kCustom, calls=%fused_computation.1 | custom fusion | bytes 1313280 | tf_op jit(solution)/shard_map/gather | solution.py:34
  37.0 2.1 %broadcast_select_fusion.1 = (bf16[16,40,512]{2,1,0:T(8,128)(2,1)}, bf16[16,40,512]{2,1,0:T(8,128)(2,1)S(1)}) fusion(bf16[16,40,512]{2,1,0:T(8,128)(2,1)} %bitcast.42, pred[16,40]{1,0:T(8,128)(4,1)S(1)} %broadcast_in_dim.53, bf16[16,40,512]{2,1,0:T(8,128)(2,1)S(1)} %bitcast.41), kind=kLoop, calls=%fused_computation.31 | loop fusion | flops 655360 | bytes 2622080 | tf_op jit(solution)/shard_map/jit(_where)/select_n | solution.py:34
  39.1 25.7 %all_to_all.31 = bf16[16,40,512]{2,1,0:T(8,128)(2,1)S(1)} all-to-all(bf16[16,40,512]{2,1,0:T(8,128)(2,1)S(1)} %get-tuple-element.21), channel_id=1, replica_groups=mesh['expert'=16,'fsdp'=2] {'expert'}, dimensions={0} | all-to-all | bytes 1310720 | tf_op jit(solution)/shard_map/all_to_all | solution.py:79
  64.9 3.6 %all-to-all-start.1 = ((bf16[16,40,512]{2,1,0:T(8,128)(2,1)}), bf16[16,40,512]{2,1,0:T(8,128)(2,1)S(1)}, u32[]{:S(2)}, u32[]{:S(2)}) async-start(bf16[16,40,512]{2,1,0:T(8,128)(2,1)} %get-tuple-element.20), calls=%async_computation.1 | async-start | bytes 1310720 | tf_op jit(solution)/shard_map/all_to_all | solution.py:82
  68.6 3.8 %fusion.12 = f32[640,2048]{1,0:T(8,128)} fusion(bf16[640,512]{1,0:T(8,128)(2,1)S(1)} %bitcast.39, bf16[1,512,2048]{2,1,0:T(8,128)(2,1)S(1)} %copy-done), kind=kOutput, calls=%fused_computation.25 | convolution fusion | flops 1342177280 | bytes 7995392 | tf_op jit(solution)/shard_map/dot_general | solution.py:40
  72.4 12.5 %all-to-all-done.1 = bf16[16,40,512]{2,1,0:T(8,128)(2,1)S(1)} async-done(((bf16[16,40,512]{2,1,0:T(8,128)(2,1)}), bf16[16,40,512]{2,1,0:T(8,128)(2,1)S(1)}, u32[]{:S(2)}, u32[]{:S(2)}) %all-to-all-start.1) | async-done | bytes 655392 | tf_op jit(solution)/shard_map/all_to_all | solution.py:82
  84.9 8.3 %multiply_reduce_fusion = (bf16[640]{0:T(1024)(128)(2,1)S(1)}, bf16[640,2048]{1,0:T(8,128)(2,1)}) fusion(f32[640,2048]{1,0:T(8,128)} %fusion.12, f32[640]{0:T(1024)S(1)} %reshape.138, bf16[640,512]{1,0:T(8,128)(2,1)S(1)} %bitcast.43, bf16[1,512,2048]{2,1,0:T(8,128)(2,1)} %param.11), kind=kOutput, calls=%fused_computation.16 | convolution fusion | flops 1372323200 | bytes 10620672 | tf_op jit(solution)/shard_map/dot_general | solution.py:41
  93.2 0.7 convert_element_type.65
  93.9 4.5 %all-to-all-start.4 = ((bf16[16,1,40]{2,1,0:T(2,128)(2,1)}), bf16[16,1,40]{2,1,0:T(2,128)(2,1)S(1)}, u32[]{:S(2)}, u32[]{:S(2)}) async-start(bf16[16,1,40]{2,1,0:T(2,128)(2,1)} %convert_element_type.65), calls=%async_computation.5 | async-start | bytes 16384 | tf_op jit(solution)/shard_map/all_to_all | solution.py:105
  98.4 4.1 %fusion.16 = bf16[640,512]{1,0:T(8,128)(2,1)} fusion(bf16[640,2048]{1,0:T(8,128)(2,1)} %get-tuple-element.19, bf16[1,512,2048]{2,1,0:T(8,128)(2,1)S(1)} %copy-done), kind=kOutput, calls=%fused_computation.29 | convolution fusion | flops 1342504960 | bytes 5373952 | tf_op jit(solution)/shard_map/dot_general | solution.py:48
  102.6 3.1 %all-to-all-done.4 = bf16[16,1,40]{2,1,0:T(2,128)(2,1)S(1)} async-done(((bf16[16,1,40]{2,1,0:T(2,128)(2,1)}), bf16[16,1,40]{2,1,0:T(2,128)(2,1)S(1)}, u32[]{:S(2)}, u32[]{:S(2)}) %all-to-all-start.4) | async-done | bytes 1312 | tf_op jit(solution)/shard_map/all_to_all | solution.py:105
  105.7 3.8 %all-to-all-start.3 = ((bf16[16,40,512]{2,1,0:T(8,128)(2,1)}), bf16[16,40,512]{2,1,0:T(8,128)(2,1)S(1)}, u32[]{:S(2)}, u32[]{:S(2)}) async-start(bf16[16,40,512]{2,1,0:T(8,128)(2,1)} %bitcast.45), calls=%async_computation.3 | async-start | bytes 1310720 | tf_op jit(solution)/shard_map/all_to_all | solution.py:98
  109.7 3.5 %gather_fusion.4 = bf16[512]{0:T(512)(128)(2,1)S(1)} fusion(bf16[640]{0:T(1024)(128)(2,1)S(1)} %reshape.137, s32[1024]{0:T(1024)S(1)} %pad_clamp_fusion), kind=kCustom, calls=%fused_computation.4 | custom fusion | bytes 4096 | tf_op jit(solution)/shard_map/gather | solution.py:116
  113.2 0.8 gather.31
  114.3 11.4 %all-to-all-done.3 = bf16[16,40,512]{2,1,0:T(8,128)(2,1)S(1)} async-done(((bf16[16,40,512]{2,1,0:T(8,128)(2,1)}), bf16[16,40,512]{2,1,0:T(8,128)(2,1)S(1)}, u32[]{:S(2)}, u32[]{:S(2)}) %all-to-all-start.3) | async-done | bytes 655392 | tf_op jit(solution)/shard_map/all_to_all | solution.py:98
  125.7 2.6 %gather_fusion.3 = bf16[512,512]{1,0:T(8,128)(2,1)} fusion(bf16[640,512]{1,0:T(8,128)(2,1)S(1)} %bitcast.38, s32[1024]{0:T(1024)S(1)} %pad_clamp_fusion), kind=kCustom, calls=%fused_computation.3 | custom fusion | bytes 1050624 | tf_op jit(solution)/shard_map/gather | solution.py:110
  128.3 1.2 gather.29
  129.6 2.1 %reduce_sum.34 = bf16[256,512]{1,0:T(8,128)(2,1)} reduce(bf16[256,2,512]{2,1,0:T(2,128)(2,1)S(1)} %gather.29, bf16[]{:T(256)} %constant.11.clone.1), dimensions={1}, to_apply=%region_2.3 | reduce | flops 131072 | bytes 786434 | tf_op jit(solution)/shard_map/reduce_sum | solution.py:114
  131.7 6.7 %fusion.8 = bf16[1,512,2048]{2,1,0:T(8,128)(2,1)} fusion(bf16[640,512]{1,0:T(8,128)(2,1)} %bitcast.44, f32[640]{0:T(1024)S(1)} %reshape.138, f32[640,2048]{1,0:T(8,128)} %fusion.12), kind=kOutput, calls=%fused_computation.21 | convolution fusion | flops 1356333056 | bytes 7997952 | tf_op jit(solution)/shard_map/dot_general | solution.py:46
  138.4 3.2 %fusion.7 = bf16[1,512,2048]{2,1,0:T(8,128)(2,1)} fusion(bf16[640,512]{1,0:T(8,128)(2,1)S(1)} %bitcast.40, bf16[640,2048]{1,0:T(8,128)(2,1)S(1)} %copy-done.1), kind=kOutput, calls=%fused_computation.20 | convolution fusion | flops 1343225856 | bytes 5373952 | tf_op jit(solution)/shard_map/dot_general | solution.py:47
  141.6 1.4 copy.25
  (34 shorter events, 1.3 us)
Async XLA Ops:
  7.2 61.4 %copy-start = (bf16[1,512,2048]{2,1,0:T(8,128)(2,1)S(1)}, bf16[1,512,2048]{2,1,0:T(8,128)(2,1)}, u32[]{:S(2)}) copy-start(bf16[1,512,2048]{2,1,0:T(8,128)(2,1)} %param.10) | copy-start | bytes 6291460
  18.1 21.0 %all-to-all-start = ((bf16[16,1,40]{2,1,0:T(2,128)(2,1)}), bf16[16,1,40]{2,1,0:T(2,128)(2,1)S(1)}, u32[]{:S(2)}, u32[]{:S(2)}) async-start(bf16[16,1,40]{2,1,0:T(2,128)(2,1)} %all_to_all.25), calls=%async_computation | async-start | bytes 16384 | tf_op jit(solution)/shard_map/all_to_all | solution.py:85
  64.9 20.1 %all-to-all-start.1 = ((bf16[16,40,512]{2,1,0:T(8,128)(2,1)}), bf16[16,40,512]{2,1,0:T(8,128)(2,1)S(1)}, u32[]{:S(2)}, u32[]{:S(2)}) async-start(bf16[16,40,512]{2,1,0:T(8,128)(2,1)} %get-tuple-element.20), calls=%async_computation.1 | async-start | bytes 1310720 | tf_op jit(solution)/shard_map/all_to_all | solution.py:82
  84.9 8.3 %copy-start.2 = (bf16[16,40,512]{2,1,0:T(8,128)(2,1)}, bf16[16,40,512]{2,1,0:T(8,128)(2,1)S(1)}, u32[]{:S(2)}) copy-start(bf16[16,40,512]{2,1,0:T(8,128)(2,1)S(1)} %all-to-all-done.1) | copy-start | bytes 1966084
  93.9 11.7 %all-to-all-start.4 = ((bf16[16,1,40]{2,1,0:T(2,128)(2,1)}), bf16[16,1,40]{2,1,0:T(2,128)(2,1)S(1)}, u32[]{:S(2)}, u32[]{:S(2)}) async-start(bf16[16,1,40]{2,1,0:T(2,128)(2,1)} %convert_element_type.65), calls=%async_computation.5 | async-start | bytes 16384 | tf_op jit(solution)/shard_map/all_to_all | solution.py:105
  105.7 20.0 %all-to-all-start.3 = ((bf16[16,40,512]{2,1,0:T(8,128)(2,1)}), bf16[16,40,512]{2,1,0:T(8,128)(2,1)S(1)}, u32[]{:S(2)}, u32[]{:S(2)}) async-start(bf16[16,40,512]{2,1,0:T(8,128)(2,1)} %bitcast.45), calls=%async_computation.3 | async-start | bytes 1310720 | tf_op jit(solution)/shard_map/all_to_all | solution.py:98
  109.5 32.1 %reduce-scatter.5.cloned.1.call-start = ((), (), s32[]{:S(2)}) async-start(), calls=%async_computation.8 | async-start | bytes 98304 | tf_op jit(solution)/shard_map/reduce_scatter | solution.py:122
  114.0 28.9 %reduce-scatter.3.cloned.1.call-start = ((), (), s32[]{:S(2)}) async-start(), calls=%async_computation.7 | async-start | bytes 393216 | tf_op jit(solution)/shard_map/reduce_scatter | solution.py:119
  131.7 6.7 %copy-start.1 = (bf16[640,2048]{1,0:T(8,128)(2,1)S(1)}, bf16[640,2048]{1,0:T(8,128)(2,1)}, u32[]{:S(2)}) copy-start(bf16[640,2048]{1,0:T(8,128)(2,1)} %get-tuple-element.19) | copy-start | bytes 7864324
Sparse Core Ops, SparseCore 0:
  114.1 8.8 reduce-scatter.4
  131.8 6.2 reduce-scatter.2
where the time goes:
time: 151 us; the launch traced here: 150 us
  blocking collectives  30.1 us (20%)
  waiting for transfers between devices  27.1 us (18%)
  local copies, waits for them, and re-layouts  26.4 us (17%)
  matrix products  26.2 us (17%)
  starting transfers between devices  20.5 us (14%)
  between operations  14.3 us (9%)
  other arithmetic  5.25 us (3%)
    all_to_all x1, blocking collectives, per_device(): lax.all_to_all(x_buf.reshape(experts, span, width), 'expert', split_axis=...  25.7 us
    all_to_all x1, waiting for transfers between devices, per_device(): lax.all_to_all(dy_buf.reshape(experts, span, width), 'expert', split_axis...  12.5 us
    all_to_all x1, waiting for transfers between devices, per_device(): lax.all_to_all(token_part.reshape(experts, span, width), 'expert', split_...  11.4 us
    all_to_all x1, starting transfers between devices, per_device(): lax.all_to_all(gate_buf.reshape(experts, span), 'expert', split_axis=0, c...  8.34 us
    dot_general x1, matrix products, expert_work(): grad_act = jnp.dot(dy_rows, out_shard, preferred_element_type=jnp.float32)  8.34 us
    dot_general x1, matrix products, expert_work(): lax.dot_general(dy_rows, act_scaled, ROW_DIMS, preferred_element_type=jnp...  6.72 us
    all_to_all x1, starting transfers between devices, per_device(): lax.all_to_all(gate_part.reshape(experts, span), 'expert', split_axis=0,...  4.47 us
    gather x2, local copies, waits for them, and re-layouts, per_device(): gate_back.reshape(total_rows)[target].astype(jnp.float32)  4.31 us
  transfers between devices with their start and end apart: 6, of which 3 were waited for; matrix products, arithmetic and copies ran while one was open for 25% of the time, Pallas kernels for 0%

commit v1 on v0

--- a/solution.py
+++ b/solution.py
@@ -7,6 +7,28 @@
 CUBIC = 0.044715
 ROW_DIMS = (((0,), (0,)), ((), ()))
 LAST_DIMS = (((1,), (1,)), ((), ()))
+
+
+def cut_along(value, dim, length):
+    before, after = (value.shape[:dim], value.shape[dim + 1 :])
+    return jnp.moveaxis(value.reshape(*before, length, -1, *after), dim, 0)
+
+
+def in_order(blocks, dim):
+    shape = list(blocks.shape[1:])
+    shape[dim] *= blocks.shape[0]
+    return jnp.moveaxis(blocks, 0, dim).reshape(shape)
+
+
+def exchange_in_pairs(value, axis, split_dim, concat_dim):
+    size, here = (lax.axis_size(axis), lax.axis_index(axis))
+    blocks = cut_along(value, split_dim, size)
+    gathered = [blocks[here]]
+    for step in range(1, size):
+        sent = blocks[here ^ step]
+        gathered.append(lax.ppermute(sent, axis, [(i, i ^ step) for i in range(size)]))
+    blocks = jnp.stack(gathered)[here ^ jnp.arange(size)]
+    return in_order(blocks, concat_dim)
 
 
 def gelu_parts(pre_act):
@@ -102,9 +124,7 @@
             concat_axis=0,
             tiled=True,
         ),
-        lax.all_to_all(
-            gate_part.reshape(experts, span), "expert", split_axis=0, concat_axis=0, tiled=True
-        ),
+        exchange_in_pairs(gate_part.reshape(experts, span), "expert", 0, 0),
     )
     token_pick = (
         token_back.reshape(total_rows, width)[target]

time: 151 us -> 163 us (1.079)
  starting transfers between devices: 20.5 us -> 44.7 us
  waiting for transfers between devices: 27.1 us -> 18.1 us
  matrix products: 26.2 us -> 23.4 us
    ppermute x0 -> x15, starting transfers between devices: none -> 28 us  [exchange_in_pairs(): lax.ppermute(sent, axis, [(i, i ^ step) for i in range(size)])]
    all_to_all x1, waiting for transfers between devices: 11.4 us -> 0.01 us  [per_device(): lax.all_to_all(token_part.reshape(experts, span, width), 'expert', split_...]
    ppermute x0 -> x15, waiting for transfers between devices: none -> 5.57 us  [exchange_in_pairs(): lax.ppermute(sent, axis, [(i, i ^ step) for i in range(size)])]
    all_to_all x1 -> x0, starting transfers between devices: 4.47 us -> none  [per_device(): lax.all_to_all(gate_part.reshape(experts, span), 'expert', split_axis=0,...]
    all_to_all x1 -> x0, waiting for transfers between devices: 3.1 us -> none  [per_device(): lax.all_to_all(gate_part.reshape(experts, span), 'expert', split_axis=0,...]
    dot_general x1, matrix products: 4.13 us -> 2.46 us  [expert_work(): lax.dot_general(grad_pre, in_shard, LAST_DIMS, preferred_element_type=jnp...]
  transfers between devices with their start and end apart: 6 -> 20, of which waited for: 3 -> 3; matrix products, arithmetic and copies ran while one was open for 25% -> 21% of each run, Pallas kernels for 0% -> 0%
where the time goes in v1:
time: 163 us
  starting transfers between devices  44.7 us (27%)
  blocking collectives  30.1 us (18%)
  local copies, waits for them, and re-layouts  26.6 us (16%)
  matrix products  23.4 us (14%)
  waiting for transfers between devices  18.1 us (11%)
  between operations  14.4 us (9%)
  other arithmetic  5.25 us (3%)
    ppermute x15, starting transfers between devices, exchange_in_pairs(): lax.ppermute(sent, axis, [(i, i ^ step) for i in range(size)])  28 us
    all_to_all x1, blocking collectives, per_device(): lax.all_to_all(x_buf.reshape(experts, span, width), 'expert', split_axis=...  25.7 us
    all_to_all x1, waiting for transfers between devices, per_device(): lax.all_to_all(dy_buf.reshape(experts, span, width), 'expert', split_axis...  12.5 us
    all_to_all x1, starting transfers between devices, per_device(): lax.all_to_all(gate_buf.reshape(experts, span), 'expert', split_axis=0, c...  8.34 us
    dot_general x1, matrix products, expert_work(): grad_act = jnp.dot(dy_rows, out_shard, preferred_element_type=jnp.float32)  7.25 us
    dot_general x1, matrix products, expert_work(): lax.dot_general(dy_rows, act_scaled, ROW_DIMS, preferred_element_type=jnp...  6.72 us
    ppermute x15, waiting for transfers between devices, exchange_in_pairs(): lax.ppermute(sent, axis, [(i, i ^ step) for i in range(size)])  5.57 us
    all_to_all x1, starting transfers between devices, per_device(): lax.all_to_all(token_part.reshape(experts, span, width), 'expert', split_...  4.48 us
  transfers between devices with their start and end apart: 20, of which 3 were waited for; matrix products, arithmetic and copies ran while one was open for 21% of the time, Pallas kernels for 0%

profile of v1, /device:TPU:0, one launch (start us, length us, event | category | flops | bytes accessed | tf_op | source)
XLA Modules:
  0.0 162.6 jit_solution(15578848359174255234)
XLA Ops:
  9.6 2.4 %scatter_custom_fusion = s32[640]{0:T(1024)S(1)} fusion(s32[512]{0:T(512)S(1)} %bitcast.126, s32[512]{0:T(512)S(1)} %iota.26, s32[]{:T(128)} %constant.31.clone.1), kind=kCustom, calls=%fused_computation.69 | custom fusion | bytes 2564 | tf_op jit(solution)/shard_map/scatter | solution.py:96
  13.1 4.3 %gather_fusion = bf16[640]{0:T(1024)(128)(2,1)S(1)} fusion(bf16[512]{0:T(512)(128)(2,1)S(1)} %reshape_reshape.7, s32[1024]{0:T(1024)S(1)} %pad_clamp_fusion.3), kind=kCustom, calls=%fused_computation | custom fusion | bytes 5120 | tf_op jit(solution)/shard_map/gather | solution.py:57
  18.1 8.3 %all-to-all-start = ((bf16[16,1,40]{2,1,0:T(2,128)(2,1)}), bf16[16,1,40]{2,1,0:T(2,128)(2,1)S(1)}, u32[]{:S(2)}, u32[]{:S(2)}) async-start(bf16[16,1,40]{2,1,0:T(2,128)(2,1)} %all_to_all.20), calls=%async_computation | async-start | bytes 16384 | tf_op jit(solution)/shard_map/all_to_all | solution.py:107
  26.6 2.2 %all_gather.7 = bf16[256,512]{1,0:T(8,128)(2,1)S(1)} all-gather(bf16[128,512]{1,0:T(8,128)(2,1)} %param.6), channel_id=1, replica_groups=mesh['expert'=16,'fsdp'=2] {'fsdp'}, dimensions={0}, use_global_device_ids=true | all-gather | bytes 393216 | tf_op jit(solution)/shard_map/all_gather | solution.py:88
  28.8 2.2 %all_gather.6 = bf16[256,512]{1,0:T(8,128)(2,1)S(1)} all-gather(bf16[128,512]{1,0:T(8,128)(2,1)} %param.7), channel_id=1, replica_groups=mesh['expert'=16,'fsdp'=2] {'fsdp'}, dimensions={0}, use_global_device_ids=true | all-gather | bytes 393216 | tf_op jit(solution)/shard_map/all_gather | solution.py:89
  31.0 2.8 %gather_fusion.2 = bf16[640,512]{1,0:T(8,128)(2,1)S(1)} fusion(bf16[256,512]{1,0:T(8,128)(2,1)S(1)} %all_gather.7, s32[1024]{0:T(1024)S(1)} %pad_clamp_fusion.2), kind=kCustom, calls=%fused_computation.2 | custom fusion | bytes 1313280 | tf_op jit(solution)/shard_map/gather | solution.py:55
  33.7 3.3 %gather_fusion.1 = bf16[640,512]{1,0:T(8,128)(2,1)} fusion(bf16[256,512]{1,0:T(8,128)(2,1)S(1)} %all_gather.6, s32[1024]{0:T(1024)S(1)} %pad_clamp_fusion.2), kind=kCustom, calls=%fused_computation.1 | custom fusion | bytes 1313280 | tf_op jit(solution)/shard_map/gather | solution.py:56
  37.0 2.1 %broadcast_select_fusion.1 = (bf16[16,40,512]{2,1,0:T(8,128)(2,1)}, bf16[16,40,512]{2,1,0:T(8,128)(2,1)S(1)}) fusion(bf16[16,40,512]{2,1,0:T(8,128)(2,1)} %bitcast.120, pred[16,40]{1,0:T(8,128)(4,1)S(1)} %broadcast_in_dim.54, bf16[16,40,512]{2,1,0:T(8,128)(2,1)S(1)} %bitcast.119), kind=kLoop, calls=%fused_computation.32 | loop fusion | flops 655360 | bytes 2622080 | tf_op jit(solution)/shard_map/jit(_where)/select_n | solution.py:56
  39.1 25.7 %all_to_all.25 = bf16[16,40,512]{2,1,0:T(8,128)(2,1)S(1)} all-to-all(bf16[16,40,512]{2,1,0:T(8,128)(2,1)S(1)} %get-tuple-element.37), channel_id=1, replica_groups=mesh['expert'=16,'fsdp'=2] {'expert'}, dimensions={0} | all-to-all | bytes 1310720 | tf_op jit(solution)/shard_map/all_to_all | solution.py:101
  64.9 3.6 %all-to-all-start.1 = ((bf16[16,40,512]{2,1,0:T(8,128)(2,1)}), bf16[16,40,512]{2,1,0:T(8,128)(2,1)S(1)}, u32[]{:S(2)}, u32[]{:S(2)}) async-start(bf16[16,40,512]{2,1,0:T(8,128)(2,1)} %get-tuple-element.36), calls=%async_computation.1 | async-start | bytes 1310720 | tf_op jit(solution)/shard_map/all_to_all | solution.py:104
  68.6 3.8 %fusion.12 = f32[640,2048]{1,0:T(8,128)} fusion(bf16[640,512]{1,0:T(8,128)(2,1)S(1)} %bitcast.117, bf16[1,512,2048]{2,1,0:T(8,128)(2,1)S(1)} %copy-done), kind=kOutput, calls=%fused_computation.26 | convolution fusion | flops 1342177280 | bytes 7995392 | tf_op jit(solution)/shard_map/dot_general | solution.py:62
  72.4 12.5 %all-to-all-done.1 = bf16[16,40,512]{2,1,0:T(8,128)(2,1)S(1)} async-done(((bf16[16,40,512]{2,1,0:T(8,128)(2,1)}), bf16[16,40,512]{2,1,0:T(8,128)(2,1)S(1)}, u32[]{:S(2)}, u32[]{:S(2)}) %all-to-all-start.1) | async-done | bytes 655392 | tf_op jit(solution)/shard_map/all_to_all | solution.py:104
  84.9 7.3 %multiply_reduce_fusion = (bf16[640]{0:T(1024)(128)(2,1)S(1)}, bf16[640,2048]{1,0:T(8,128)(2,1)S(1)}) fusion(f32[640,2048]{1,0:T(8,128)} %fusion.12, f32[640]{0:T(1024)S(1)} %reshape.145, bf16[640,512]{1,0:T(8,128)(2,1)S(1)} %bitcast.121, bf16[1,512,2048]{2,1,0:T(8,128)(2,1)} %param.11), kind=kOutput, calls=%fused_computation.17 | convolution fusion | flops 1372323200 | bytes 10620672 | tf_op jit(solution)/shard_map/dot_general | solution.py:63
  92.2 2.5 %fusion.16 = bf16[640,512]{1,0:T(8,128)(2,1)} fusion(bf16[640,2048]{1,0:T(8,128)(2,1)S(1)} %get-tuple-element.19, bf16[1,512,2048]{2,1,0:T(8,128)(2,1)S(1)} %copy-done), kind=kOutput, calls=%fused_computation.30 | convolution fusion | flops 1342504960 | bytes 5373952 | tf_op jit(solution)/shard_map/dot_general | solution.py:70
  94.7 4.5 %all-to-all-start.3 = ((bf16[16,40,512]{2,1,0:T(8,128)(2,1)}), bf16[16,40,512]{2,1,0:T(8,128)(2,1)S(1)}, u32[]{:S(2)}, u32[]{:S(2)}) async-start(bf16[16,40,512]{2,1,0:T(8,128)(2,1)} %bitcast.123), calls=%async_computation.3 | async-start | bytes 1310720 | tf_op jit(solution)/shard_map/all_to_all | solution.py:120
  99.7 2.0 %collective-permute-start = (bf16[1,40]{1,0:T(2,128)(2,1)S(1)}, bf16[1,40]{1,0:T(2,128)(2,1)S(1)}, u32[]{:S(2)}, u32[]{:S(2)}) collective-permute-start(bf16[1,40]{1,0:T(2,128)(2,1)S(1)} %get-tuple-element.34), channel_id=1, source_target_pairs={{0,2},{2,0},{4,6},{6,4},{8,10},{10,8},{12,14},{14,12},{16,18},{18,... | collective-permute-start | bytes 248 | tf_op jit(solution)/shard_map/ppermute | solution.py:29
  103.2 1.9 %collective-permute-start.3 = (bf16[1,40]{1,0:T(2,128)(2,1)S(1)}, bf16[1,40]{1,0:T(2,128)(2,1)S(1)}, u32[]{:S(2)}, u32[]{:S(2)}) collective-permute-start(bf16[1,40]{1,0:T(2,128)(2,1)S(1)} %get-tuple-element.31), channel_id=1, source_target_pairs={{0,8},{2,10},{4,12},{6,14},{8,0},{10,2},{12,4},{14,6},{16,24},{18,... | collective-permute-start | bytes 248 | tf_op jit(solution)/shard_map/ppermute | solution.py:29
  106.6 2.4 %collective-permute-start.5 = (bf16[1,40]{1,0:T(2,128)(2,1)S(1)}, bf16[1,40]{1,0:T(2,128)(2,1)S(1)}, u32[]{:S(2)}, u32[]{:S(2)}) collective-permute-start(bf16[1,40]{1,0:T(2,128)(2,1)S(1)} %get-tuple-element.29), channel_id=1, source_target_pairs={{0,12},{2,14},{4,8},{6,10},{8,4},{10,6},{12,0},{14,2},{16,28},{18,... | collective-permute-start | bytes 248 | tf_op jit(solution)/shard_map/ppermute | solution.py:29
  109.1 2.8 %collective-permute-start.7 = (bf16[1,40]{1,0:T(2,128)(2,1)S(1)}, bf16[1,40]{1,0:T(2,128)(2,1)S(1)}, u32[]{:S(2)}, u32[]{:S(2)}) collective-permute-start(bf16[1,40]{1,0:T(2,128)(2,1)S(1)} %get-tuple-element.27), channel_id=1, source_target_pairs={{0,16},{2,18},{4,20},{6,22},{8,24},{10,26},{12,28},{14,30},{16,0},... | collective-permute-start | bytes 248 | tf_op jit(solution)/shard_map/ppermute | solution.py:29
  111.9 2.5 %collective-permute-start.8 = (bf16[1,40]{1,0:T(2,128)(2,1)S(1)}, bf16[1,40]{1,0:T(2,128)(2,1)S(1)}, u32[]{:S(2)}, u32[]{:S(2)}) collective-permute-start(bf16[1,40]{1,0:T(2,128)(2,1)S(1)} %get-tuple-element.26), channel_id=1, source_target_pairs={{0,18},{2,16},{4,22},{6,20},{8,26},{10,24},{12,30},{14,28},{16,2},... | collective-permute-start | bytes 248 | tf_op jit(solution)/shard_map/ppermute | solution.py:29
  114.5 2.2 %collective-permute-start.9 = (bf16[1,40]{1,0:T(2,128)(2,1)S(1)}, bf16[1,40]{1,0:T(2,128)(2,1)S(1)}, u32[]{:S(2)}, u32[]{:S(2)}) collective-permute-start(bf16[1,40]{1,0:T(2,128)(2,1)S(1)} %get-tuple-element.25), channel_id=1, source_target_pairs={{0,20},{2,22},{4,16},{6,18},{8,28},{10,30},{12,24},{14,26},{16,4},... | collective-permute-start | bytes 248 | tf_op jit(solution)/shard_map/ppermute | solution.py:29
  116.7 1.6 collective-permute-start.10
  118.3 2.2 %collective-permute-start.11 = (bf16[1,40]{1,0:T(2,128)(2,1)S(1)}, bf16[1,40]{1,0:T(2,128)(2,1)S(1)}, u32[]{:S(2)}, u32[]{:S(2)}) collective-permute-start(bf16[1,40]{1,0:T(2,128)(2,1)S(1)} %get-tuple-element.23), channel_id=1, source_target_pairs={{0,24},{2,26},{4,28},{6,30},{8,16},{10,18},{12,20},{14,22},{16,8},... | collective-permute-start | bytes 248 | tf_op jit(solution)/shard_map/ppermute | solution.py:29
  120.5 2.5 %collective-permute-start.12 = (bf16[1,40]{1,0:T(2,128)(2,1)S(1)}, bf16[1,40]{1,0:T(2,128)(2,1)S(1)}, u32[]{:S(2)}, u32[]{:S(2)}) collective-permute-start(bf16[1,40]{1,0:T(2,128)(2,1)S(1)} %get-tuple-element.22), channel_id=1, source_target_pairs={{0,26},{2,24},{4,30},{6,28},{8,18},{10,16},{12,22},{14,20},{16,10}... | collective-permute-start | bytes 248 | tf_op jit(solution)/shard_map/ppermute | solution.py:29
  123.0 3.1 %collective-permute-start.13 = (bf16[1,40]{1,0:T(2,128)(2,1)S(1)}, bf16[1,40]{1,0:T(2,128)(2,1)S(1)}, u32[]{:S(2)}, u32[]{:S(2)}) collective-permute-start(bf16[1,40]{1,0:T(2,128)(2,1)S(1)} %get-tuple-element.21), channel_id=1, source_target_pairs={{0,28},{2,30},{4,24},{6,26},{8,20},{10,22},{12,16},{14,18},{16,12}... | collective-permute-start | bytes 248 | tf_op jit(solution)/shard_map/ppermute | solution.py:29
  126.1 1.6 collective-permute-start.14
  129.3 4.0 %collective-permute-done.14 = bf16[1,40]{1,0:T(2,128)(2,1)S(1)} collective-permute-done((bf16[1,40]{1,0:T(2,128)(2,1)S(1)}, bf16[1,40]{1,0:T(2,128)(2,1)S(1)}, u32[]{:S(2)}, u32[]{:S(2)}) %collective-permute-start.14) | collective-permute-done | bytes 112 | tf_op jit(solution)/shard_map/ppermute | solution.py:29
  134.0 3.5 %gather_fusion.5 = bf16[512]{0:T(512)(128)(2,1)S(1)} fusion(bf16[640]{0:T(1024)(128)(2,1)S(1)} %reshape_reshape.8, s32[1024]{0:T(1024)S(1)} %pad_clamp_fusion.1), kind=kCustom, calls=%fused_computation.5 | custom fusion | bytes 4096 | tf_op jit(solution)/shard_map/gather | solution.py:136
  138.4 2.6 %gather_fusion.3 = bf16[512,512]{1,0:T(8,128)(2,1)} fusion(bf16[640,512]{1,0:T(8,128)(2,1)S(1)} %bitcast.116, s32[1024]{0:T(1024)S(1)} %pad_clamp_fusion.1), kind=kCustom, calls=%fused_computation.3 | custom fusion | bytes 1050624 | tf_op jit(solution)/shard_map/gather | solution.py:130
  142.3 2.1 %reduce_sum.34 = bf16[256,512]{1,0:T(8,128)(2,1)} reduce(bf16[256,2,512]{2,1,0:T(2,128)(2,1)S(1)} %gather.32, bf16[]{:T(256)} %constant.37.clone.1), dimensions={1}, to_apply=%region_2.3 | reduce | flops 131072 | bytes 786434 | tf_op jit(solution)/shard_map/reduce_sum | solution.py:134
  144.4 6.7 %fusion.8 = bf16[1,512,2048]{2,1,0:T(8,128)(2,1)} fusion(bf16[640,512]{1,0:T(8,128)(2,1)} %bitcast.122, f32[640]{0:T(1024)S(1)} %reshape.145, f32[640,2048]{1,0:T(8,128)} %fusion.12), kind=kOutput, calls=%fused_computation.22 | convolution fusion | flops 1356333056 | bytes 7997952 | tf_op jit(solution)/shard_map/dot_general | solution.py:68
  151.2 3.2 %fusion.7 = bf16[1,512,2048]{2,1,0:T(8,128)(2,1)} fusion(bf16[640,512]{1,0:T(8,128)(2,1)S(1)} %bitcast.118, bf16[640,2048]{1,0:T(8,128)(2,1)S(1)} %copy-done.2), kind=kOutput, calls=%fused_computation.21 | convolution fusion | flops 1343225856 | bytes 5373952 | tf_op jit(solution)/shard_map/dot_general | solution.py:69
  (68 shorter events, 13.7 us)
Async XLA Ops:
  7.2 61.4 %copy-start = (bf16[1,512,2048]{2,1,0:T(8,128)(2,1)S(1)}, bf16[1,512,2048]{2,1,0:T(8,128)(2,1)}, u32[]{:S(2)}) copy-start(bf16[1,512,2048]{2,1,0:T(8,128)(2,1)} %param.10) | copy-start | bytes 6291460
  18.1 21.0 %all-to-all-start = ((bf16[16,1,40]{2,1,0:T(2,128)(2,1)}), bf16[16,1,40]{2,1,0:T(2,128)(2,1)S(1)}, u32[]{:S(2)}, u32[]{:S(2)}) async-start(bf16[16,1,40]{2,1,0:T(2,128)(2,1)} %all_to_all.20), calls=%async_computation | async-start | bytes 16384 | tf_op jit(solution)/shard_map/all_to_all | solution.py:107
  64.9 20.1 %all-to-all-start.1 = ((bf16[16,40,512]{2,1,0:T(8,128)(2,1)}), bf16[16,40,512]{2,1,0:T(8,128)(2,1)S(1)}, u32[]{:S(2)}, u32[]{:S(2)}) async-start(bf16[16,40,512]{2,1,0:T(8,128)(2,1)} %get-tuple-element.36), calls=%async_computation.1 | async-start | bytes 1310720 | tf_op jit(solution)/shard_map/all_to_all | solution.py:104
  84.9 7.3 %copy-start.3 = (bf16[16,40,512]{2,1,0:T(8,128)(2,1)}, bf16[16,40,512]{2,1,0:T(8,128)(2,1)S(1)}, u32[]{:S(2)}) copy-start(bf16[16,40,512]{2,1,0:T(8,128)(2,1)S(1)} %all-to-all-done.1) | copy-start | bytes 1966084
  92.2 2.5 %copy-start.1 = (bf16[640,2048]{1,0:T(8,128)(2,1)}, bf16[640,2048]{1,0:T(8,128)(2,1)S(1)}, u32[]{:S(2)}) copy-start(bf16[640,2048]{1,0:T(8,128)(2,1)S(1)} %get-tuple-element.19) | copy-start | bytes 7864324
  94.7 43.8 %all-to-all-start.3 = ((bf16[16,40,512]{2,1,0:T(8,128)(2,1)}), bf16[16,40,512]{2,1,0:T(8,128)(2,1)S(1)}, u32[]{:S(2)}, u32[]{:S(2)}) async-start(bf16[16,40,512]{2,1,0:T(8,128)(2,1)} %bitcast.123), calls=%async_computation.3 | async-start | bytes 1310720 | tf_op jit(solution)/shard_map/all_to_all | solution.py:120
  99.1 55.2 %reduce-scatter.5.cloned.1.call-start = ((), (), s32[]{:S(2)}) async-start(), calls=%async_computation.7 | async-start | bytes 98304 | tf_op jit(solution)/shard_map/reduce_scatter | solution.py:142
  99.7 6.9 %collective-permute-start = (bf16[1,40]{1,0:T(2,128)(2,1)S(1)}, bf16[1,40]{1,0:T(2,128)(2,1)S(1)}, u32[]{:S(2)}, u32[]{:S(2)}) collective-permute-start(bf16[1,40]{1,0:T(2,128)(2,1)S(1)} %get-tuple-element.34), channel_id=1, source_target_pairs={{0,2},{2,0},{4,6},{6,4},{8,10},{10,8},{12,14},{14,12},{16,18},{18,... | collective-permute-start | bytes 248 | tf_op jit(solution)/shard_map/ppermute | solution.py:29
  101.7 7.3 %collective-permute-start.1 = (bf16[1,40]{1,0:T(2,128)(2,1)S(1)}, bf16[1,40]{1,0:T(2,128)(2,1)S(1)}, u32[]{:S(2)}, u32[]{:S(2)}) collective-permute-start(bf16[1,40]{1,0:T(2,128)(2,1)S(1)} %get-tuple-element.33), channel_id=1, source_target_pairs={{0,4},{2,6},{4,0},{6,2},{8,12},{10,14},{12,8},{14,10},{16,20},{18,... | collective-permute-start | bytes 248 | tf_op jit(solution)/shard_map/ppermute | solution.py:29
  103.1 6.0 %collective-permute-start.2 = (bf16[1,40]{1,0:T(2,128)(2,1)S(1)}, bf16[1,40]{1,0:T(2,128)(2,1)S(1)}, u32[]{:S(2)}, u32[]{:S(2)}) collective-permute-start(bf16[1,40]{1,0:T(2,128)(2,1)S(1)} %get-tuple-element.32), channel_id=1, source_target_pairs={{0,6},{2,4},{4,2},{6,0},{8,14},{10,12},{12,10},{14,8},{16,22},{18,... | collective-permute-start | bytes 248 | tf_op jit(solution)/shard_map/ppermute | solution.py:29
  103.2 8.7 %collective-permute-start.3 = (bf16[1,40]{1,0:T(2,128)(2,1)S(1)}, bf16[1,40]{1,0:T(2,128)(2,1)S(1)}, u32[]{:S(2)}, u32[]{:S(2)}) collective-permute-start(bf16[1,40]{1,0:T(2,128)(2,1)S(1)} %get-tuple-element.31), channel_id=1, source_target_pairs={{0,8},{2,10},{4,12},{6,14},{8,0},{10,2},{12,4},{14,6},{16,24},{18,... | collective-permute-start | bytes 248 | tf_op jit(solution)/shard_map/ppermute | solution.py:29
  105.2 9.3 %collective-permute-start.4 = (bf16[1,40]{1,0:T(2,128)(2,1)S(1)}, bf16[1,40]{1,0:T(2,128)(2,1)S(1)}, u32[]{:S(2)}, u32[]{:S(2)}) collective-permute-start(bf16[1,40]{1,0:T(2,128)(2,1)S(1)} %get-tuple-element.30), channel_id=1, source_target_pairs={{0,10},{2,8},{4,14},{6,12},{8,2},{10,0},{12,6},{14,4},{16,26},{18,... | collective-permute-start | bytes 248 | tf_op jit(solution)/shard_map/ppermute | solution.py:29
  106.6 10.0 %collective-permute-start.5 = (bf16[1,40]{1,0:T(2,128)(2,1)S(1)}, bf16[1,40]{1,0:T(2,128)(2,1)S(1)}, u32[]{:S(2)}, u32[]{:S(2)}) collective-permute-start(bf16[1,40]{1,0:T(2,128)(2,1)S(1)} %get-tuple-element.29), channel_id=1, source_target_pairs={{0,12},{2,14},{4,8},{6,10},{8,4},{10,6},{12,0},{14,2},{16,28},{18,... | collective-permute-start | bytes 248 | tf_op jit(solution)/shard_map/ppermute | solution.py:29
  109.0 9.3 %collective-permute-start.6 = (bf16[1,40]{1,0:T(2,128)(2,1)S(1)}, bf16[1,40]{1,0:T(2,128)(2,1)S(1)}, u32[]{:S(2)}, u32[]{:S(2)}) collective-permute-start(bf16[1,40]{1,0:T(2,128)(2,1)S(1)} %get-tuple-element.28), channel_id=1, source_target_pairs={{0,14},{2,12},{4,10},{6,8},{8,6},{10,4},{12,2},{14,0},{16,30},{18,... | collective-permute-start | bytes 248 | tf_op jit(solution)/shard_map/ppermute | solution.py:29
  109.1 11.4 %collective-permute-start.7 = (bf16[1,40]{1,0:T(2,128)(2,1)S(1)}, bf16[1,40]{1,0:T(2,128)(2,1)S(1)}, u32[]{:S(2)}, u32[]{:S(2)}) collective-permute-start(bf16[1,40]{1,0:T(2,128)(2,1)S(1)} %get-tuple-element.27), channel_id=1, source_target_pairs={{0,16},{2,18},{4,20},{6,22},{8,24},{10,26},{12,28},{14,30},{16,0},... | collective-permute-start | bytes 248 | tf_op jit(solution)/shard_map/ppermute | solution.py:29
  111.9 11.1 %collective-permute-start.8 = (bf16[1,40]{1,0:T(2,128)(2,1)S(1)}, bf16[1,40]{1,0:T(2,128)(2,1)S(1)}, u32[]{:S(2)}, u32[]{:S(2)}) collective-permute-start(bf16[1,40]{1,0:T(2,128)(2,1)S(1)} %get-tuple-element.26), channel_id=1, source_target_pairs={{0,18},{2,16},{4,22},{6,20},{8,26},{10,24},{12,30},{14,28},{16,2},... | collective-permute-start | bytes 248 | tf_op jit(solution)/shard_map/ppermute | solution.py:29
  114.5 11.7 %collective-permute-start.9 = (bf16[1,40]{1,0:T(2,128)(2,1)S(1)}, bf16[1,40]{1,0:T(2,128)(2,1)S(1)}, u32[]{:S(2)}, u32[]{:S(2)}) collective-permute-start(bf16[1,40]{1,0:T(2,128)(2,1)S(1)} %get-tuple-element.25), channel_id=1, source_target_pairs={{0,20},{2,22},{4,16},{6,18},{8,28},{10,30},{12,24},{14,26},{16,4},... | collective-permute-start | bytes 248 | tf_op jit(solution)/shard_map/ppermute | solution.py:29
  116.7 11.1 %collective-permute-start.10 = (bf16[1,40]{1,0:T(2,128)(2,1)S(1)}, bf16[1,40]{1,0:T(2,128)(2,1)S(1)}, u32[]{:S(2)}, u32[]{:S(2)}) collective-permute-start(bf16[1,40]{1,0:T(2,128)(2,1)S(1)} %get-tuple-element.24), channel_id=1, source_target_pairs={{0,22},{2,20},{4,18},{6,16},{8,30},{10,28},{12,26},{14,24},{16,6},... | collective-permute-start | bytes 248 | tf_op jit(solution)/shard_map/ppermute | solution.py:29
  118.3 9.5 %collective-permute-start.11 = (bf16[1,40]{1,0:T(2,128)(2,1)S(1)}, bf16[1,40]{1,0:T(2,128)(2,1)S(1)}, u32[]{:S(2)}, u32[]{:S(2)}) collective-permute-start(bf16[1,40]{1,0:T(2,128)(2,1)S(1)} %get-tuple-element.23), channel_id=1, source_target_pairs={{0,24},{2,26},{4,28},{6,30},{8,16},{10,18},{12,20},{14,22},{16,8},... | collective-permute-start | bytes 248 | tf_op jit(solution)/shard_map/ppermute | solution.py:29
  120.5 7.3 %collective-permute-start.12 = (bf16[1,40]{1,0:T(2,128)(2,1)S(1)}, bf16[1,40]{1,0:T(2,128)(2,1)S(1)}, u32[]{:S(2)}, u32[]{:S(2)}) collective-permute-start(bf16[1,40]{1,0:T(2,128)(2,1)S(1)} %get-tuple-element.22), channel_id=1, source_target_pairs={{0,26},{2,24},{4,30},{6,28},{8,18},{10,16},{12,22},{14,20},{16,10}... | collective-permute-start | bytes 248 | tf_op jit(solution)/shard_map/ppermute | solution.py:29
  123.0 6.3 %collective-permute-start.13 = (bf16[1,40]{1,0:T(2,128)(2,1)S(1)}, bf16[1,40]{1,0:T(2,128)(2,1)S(1)}, u32[]{:S(2)}, u32[]{:S(2)}) collective-permute-start(bf16[1,40]{1,0:T(2,128)(2,1)S(1)} %get-tuple-element.21), channel_id=1, source_target_pairs={{0,28},{2,30},{4,24},{6,26},{8,20},{10,22},{12,16},{14,18},{16,12}... | collective-permute-start | bytes 248 | tf_op jit(solution)/shard_map/ppermute | solution.py:29
  126.1 7.2 %collective-permute-start.14 = (bf16[1,40]{1,0:T(2,128)(2,1)S(1)}, bf16[1,40]{1,0:T(2,128)(2,1)S(1)}, u32[]{:S(2)}, u32[]{:S(2)}) collective-permute-start(bf16[1,40]{1,0:T(2,128)(2,1)S(1)} %get-tuple-element.20), channel_id=1, source_target_pairs={{0,30},{2,28},{4,26},{6,24},{8,22},{10,20},{12,18},{14,16},{16,14}... | collective-permute-start | bytes 248 | tf_op jit(solution)/shard_map/ppermute | solution.py:29
  138.4 17.4 %reduce-scatter.3.cloned.1.call-start = ((), (), s32[]{:S(2)}) async-start(), calls=%async_computation.6 | async-start | bytes 393216 | tf_op jit(solution)/shard_map/reduce_scatter | solution.py:139
  144.4 6.7 %copy-start.2 = (bf16[640,2048]{1,0:T(8,128)(2,1)S(1)}, bf16[640,2048]{1,0:T(8,128)(2,1)}, u32[]{:S(2)}) copy-start(bf16[640,2048]{1,0:T(8,128)(2,1)} %copy-done.1) | copy-start | bytes 7864324
Sparse Core Ops, SparseCore 0:
  138.5 4.9 reduce-scatter.4
  146.3 8.8 reduce-scatter.2
